TPU v7x, 32 devices: a whole 2x2x4 slice. The times are simulated.
32 devices in a mesh: dp: 16 (over z, y, core), seq: 2 (over x).
Axes of the slice: x: 2, y: 2, z: 4, core: 2. Of those that a mesh axis runs over, the one named last changes fastest.
Arguments:
- hidden_in: bfloat16 [16, 1024, 768], P('dp', 'seq'), may hold values from -18 to 18
- segment_ids: int32 [16, 1024], P('dp'), may hold values from 0 to 7, as said below
- piece_lengths: int32 [16, 8], P('dp'), may hold values from 0 to 1024, as said below
- time_index: int32 [16, 8], P('dp'), may hold values from 0 to 999
- first_gain: float32 [768], replicated, may hold values from 0.5 to 1.5
- modulation_weight: bfloat16 [128, 4608], replicated, may hold values from -0.5 to 0.5
- modulation_bias: float32 [4608], replicated, may hold values from -4 to 4
- query_key_value_weight: bfloat16 [768, 2304], replicated, may hold values from -0.21875 to 0.21875
- attention_output_matrix: bfloat16 [768, 768], replicated, may hold values from -0.875 to 0.875
- second_gain: float32 [768], replicated, may hold values from 0.5 to 1.5
- widen_weight: bfloat16 [768, 3072], replicated, may hold values from -0.21875 to 0.21875
- expand_bias: float32 [3072], replicated, may hold values from -6 to 6
- narrow_weight: bfloat16 [3072, 768], replicated, may hold values from -0.109375 to 0.109375
- reduce_bias: float32 [768], replicated, may hold values from -6 to 6
- cotangent: bfloat16 [16, 1024, 768], P('dp', 'seq'), may hold values from -6 to 6
Outputs:
- block_out: bfloat16 [16, 1024, 768], P('dp', 'seq')
- input_grad: bfloat16 [16, 1024, 768], P('dp', 'seq')
- first_gain_grad: float32 [768], replicated
- modulation_weight_grad: float32 [128, 4608], P('seq', 'dp')
- modulation_bias_grad: float32 [4608], replicated
- triple_weight_grad: float32 [768, 2304], P('seq', 'dp')
- output_weight_grad: float32 [768, 768], P('seq', 'dp')
- second_gain_grad: float32 [768], replicated
- expand_weight_grad: float32 [768, 3072], P('seq', 'dp')
- expand_bias_grad: float32 [3072], replicated
- reduce_weight_grad: float32 [3072, 768], P('seq', 'dp')
- reduce_bias_grad: float32 [768], replicated
- masked_rms: float32 [3], replicated
Inputs may be any that keep to these rules, and one draw needn't show every extreme that they name: `segment_ids`: each slot is cut into equal pieces of 128, 512 or 1024 tokens, the kind drawn for each slot, and a token's segment id is the number of its piece, so ids start at 0 and never fall; the first slot has pieces of 128 and the last one a single piece. piece_lengths[slot, s] counts the valid leading tokens of piece s: more than half of the piece and at most all of it, the first piece of every slot all valid; 0 for numbers beyond the slot's pieces.
All inputs are finite; a program needn't handle non-finite values.
Results may differ from a plain program's by a relative error of at most 0.014.
Values may be sent and summed in bfloat16 or wider, within the bound.
A program may use at most 192 MiB of HBM per device.

v0:
```python
import math
import jax
import jax.numpy as jnp
from jax import lax
from jax.sharding import PartitionSpec as P

HEADS = 12
highest = lax.Precision.HIGHEST
negative = -1000000000.0


def layer_norm(values, scaling):
    centered = values - jnp.mean(values, axis=-1, keepdims=True)
    spread = jnp.mean(centered * centered, axis=-1, keepdims=True)
    return centered * lax.rsqrt(spread + 1e-05) * scaling


def norm_modulate(values, scaling, offset, stretch):
    return layer_norm(values, scaling) * (1.0 + stretch) + offset


def gelu_tanh(values):
    argument = 0.7978845608028654 * (values + 0.044715 * values * values * values)
    return 0.5 * values * (1.0 + jnp.tanh(argument))


def rotate(values, cosine, sine_part):
    halfway = values.shape[-1] // 2
    turned = jnp.concatenate([-values[..., halfway:], values[..., :halfway]], axis=-1)
    return values * cosine + turned * sine_part


def rotary_tables(positions, head_dim):
    freq_index = jnp.arange(head_dim // 2).astype(jnp.float32)
    frequencies = jnp.exp(freq_index * (-2.0 * math.log(10000.0) / head_dim))
    angles = positions[..., None] * frequencies
    angles = jnp.concatenate([angles, angles], axis=-1)
    return (jnp.cos(angles)[..., None, :], jnp.sin(angles)[..., None, :])


def time_embed(time_values, feature_count):
    halfway = feature_count // 2
    freq_index = jnp.arange(halfway).astype(jnp.float32)
    frequencies = jnp.exp(freq_index * (-math.log(10000.0) / halfway))
    angles = time_values.astype(jnp.float32)[..., None] * frequencies
    return jnp.concatenate([jnp.cos(angles), jnp.sin(angles)], axis=-1)


def slot_layout(segments, lengths):
    seg_range = jnp.arange(lengths.shape[-1], dtype=jnp.int32)
    membership = (segments[..., :, None] == seg_range).astype(jnp.float32)
    piece_sizes = jnp.sum(membership, axis=-2)
    piece_starts = jnp.cumsum(piece_sizes, axis=-1) - piece_sizes
    token_start = jnp.sum(membership * piece_starts[..., None, :], axis=-1)
    positions = jnp.arange(segments.shape[-1]).astype(jnp.float32) - token_start
    valid_limit = jnp.sum(membership * lengths.astype(jnp.float32)[..., None, :], axis=-1)
    validity = (positions < valid_limit).astype(jnp.float32)
    return (membership, positions, validity)


def block_order(matrix, seq_count, data_count):
    rows, cols = matrix.shape
    arranged = matrix.reshape(seq_count, rows // seq_count, data_count, cols // data_count)
    arranged = arranged.transpose(2, 0, 1, 3)
    return arranged.reshape(data_count * rows, cols // data_count)


def local(
    hidden_in,
    segment_ids,
    piece_lengths,
    time_index,
    first_gain,
    modulation_weight,
    modulation_bias,
    query_key_value_weight,
    attention_output_matrix,
    second_gain,
    widen_weight,
    expand_bias,
    narrow_weight,
    reduce_bias,
    cotangent,
):
    slot_count, own_rows, width = hidden_in.shape
    slot_rows = segment_ids.shape[1]
    head_count = HEADS
    head_dim = width // head_count
    score_scale = head_dim ** (-0.5)
    first_row = lax.axis_index("seq") * own_rows
    membership, positions, validity = slot_layout(segment_ids, piece_lengths)
    own_member = lax.dynamic_slice_in_dim(membership, first_row, own_rows, 1)
    own_pos = lax.dynamic_slice_in_dim(positions, first_row, own_rows, 1)
    own_valid = lax.dynamic_slice_in_dim(validity, first_row, own_rows, 1)
    own_segments = lax.dynamic_slice_in_dim(segment_ids, first_row, own_rows, 1)
    allowed = (own_segments[:, :, None] == segment_ids[:, None, :]) & (validity[:, None, :] > 0.5)
    condition = time_embed(time_index, modulation_weight.shape[0]).astype(jnp.bfloat16)
    modulation = (
        jnp.einsum("smc,cf->smf", condition, modulation_weight, preferred_element_type=jnp.float32)
        + modulation_bias
    )
    per_token = jnp.zeros((slot_count, own_rows, modulation.shape[-1]), jnp.float32)
    for segment in range(membership.shape[-1]):
        per_token = (
            per_token
            + own_member[:, :, segment : segment + 1] * modulation[:, segment : segment + 1, :]
        )
    shift_attn, scale_attn, gate_attn, shift_mlp, scale_mlp, gate_mlp = jnp.split(
        per_token, 6, axis=-1
    )
    residual = hidden_in.astype(jnp.float32)
    first_normed_tokens = norm_modulate(residual, first_gain, shift_attn, scale_attn).astype(
        jnp.bfloat16
    )
    triple = jnp.einsum(
        "map,pr->mar",
        first_normed_tokens,
        query_key_value_weight,
        preferred_element_type=jnp.float32,
    )
    query, key_raw, value_raw = jnp.split(triple, 3, axis=-1)
    four_dims = (slot_count, own_rows, head_count, head_dim)
    cosine, sine_part = rotary_tables(own_pos, head_dim)

    def turn(raw_values):
        return rotate(raw_values, cosine, sine_part)

    query_turned, turn_back = jax.vjp(turn, query.reshape(four_dims))
    query_rot = query_turned.astype(jnp.bfloat16)
    key_rot = (
        turn(key_raw.reshape(four_dims)).astype(jnp.bfloat16).reshape(slot_count, own_rows, width)
    )
    value_low = value_raw.astype(jnp.bfloat16)
    all_keys, all_values = (
        lax.all_gather(key_rot, "seq", axis=1, tiled=True),
        lax.all_gather(value_low, "seq", axis=1, tiled=True),
    )
    all_keys = all_keys.reshape(slot_count, slot_rows, head_count, head_dim)
    all_values = all_values.reshape(slot_count, slot_rows, head_count, head_dim)

    def attend(inputs):
        queries, keys, values, key_mask = inputs
        scores = (
            jnp.einsum("qhd,khd->hqk", queries, keys, preferred_element_type=jnp.float32)
            * score_scale
        )
        scores = jnp.where(key_mask[None], scores, negative)
        row_peak = jnp.max(scores, axis=-1, keepdims=True)
        exponent = jnp.exp(scores - row_peak)
        row_total = jnp.sum(exponent, axis=-1, keepdims=True)
        probability = exponent / row_total
        weighted = jnp.einsum(
            "hqk,khd->qhd",
            probability.astype(jnp.bfloat16),
            values,
            preferred_element_type=jnp.float32,
        )
        return (weighted, (row_peak + jnp.log(row_total))[..., 0])

    attended, log_total = lax.map(attend, (query_rot, all_keys, all_values, allowed))
    attention_result_narrow = attended.reshape(slot_count, own_rows, width).astype(jnp.bfloat16)
    projected = jnp.einsum(
        "rkn,nh->rkh",
        attention_result_narrow,
        attention_output_matrix,
        preferred_element_type=jnp.float32,
    )
    attn_branch = gate_attn * projected
    middle = residual + attn_branch
    second_normed_tokens = norm_modulate(middle, second_gain, shift_mlp, scale_mlp).astype(
        jnp.bfloat16
    )
    expanded = (
        jnp.einsum(
            "map,pr->mar", second_normed_tokens, widen_weight, preferred_element_type=jnp.float32
        )
        + expand_bias
    )
    gelu_activations = gelu_tanh(expanded).astype(jnp.bfloat16)
    reduced = (
        jnp.einsum(
            "jpb,bc->jpc", gelu_activations, narrow_weight, preferred_element_type=jnp.float32
        )
        + reduce_bias
    )
    mlp_branch = gate_mlp * reduced
    block_value = middle + mlp_branch
    block_out = block_value.astype(jnp.bfloat16)
    masked = own_valid[..., None]
    stat_terms = jnp.stack(
        [
            jnp.sum(masked * block_value * block_value),
            jnp.sum(masked * attn_branch * attn_branch),
            jnp.sum(masked * mlp_branch * mlp_branch),
            jnp.sum(own_valid),
        ]
    )
    grad_out = cotangent.astype(jnp.float32) * masked
    grad_gate_mlp = grad_out * reduced
    gradient_narrowed = (gate_mlp * grad_out).astype(jnp.bfloat16)
    reduce_weight_grad = jnp.einsum(
        "mhg,mhn->gn", gelu_activations, gradient_narrowed, preferred_element_type=jnp.float32
    )
    reduce_bias_grad = jnp.sum(gradient_narrowed.astype(jnp.float32), axis=(0, 1))
    grad_activated = jnp.einsum(
        "kav,cv->kac", gradient_narrowed, narrow_weight, preferred_element_type=jnp.float32
    )
    gradient_widened = jax.vjp(gelu_tanh, expanded)[1](grad_activated)[0].astype(jnp.bfloat16)
    expand_weight_grad = jnp.einsum(
        "cqe,cqr->er", second_normed_tokens, gradient_widened, preferred_element_type=jnp.float32
    )
    expand_bias_grad = jnp.sum(gradient_widened.astype(jnp.float32), axis=(0, 1))
    grad_normed_two = jnp.einsum(
        "yma,ja->ymj", gradient_widened, widen_weight, preferred_element_type=jnp.float32
    )
    second_back = jax.vjp(norm_modulate, middle, second_gain, shift_mlp, scale_mlp)[1]
    grad_middle_norm, second_gain_grad, grad_shift_mlp, grad_scale_mlp = second_back(
        grad_normed_two
    )
    grad_middle = grad_out + grad_middle_norm
    grad_gate_attn = grad_middle * projected
    gradient_attention_projected = (gate_attn * grad_middle).astype(jnp.bfloat16)
    output_weight_grad = jnp.einsum(
        "grm,gra->ma",
        attention_result_narrow,
        gradient_attention_projected,
        preferred_element_type=jnp.float32,
    )
    grad_attended = (
        jnp.einsum(
            "yzq,rq->yzr",
            gradient_attention_projected,
            attention_output_matrix,
            preferred_element_type=jnp.float32,
        )
        .astype(jnp.bfloat16)
        .reshape(four_dims)
    )

    def attend_back(inputs):
        queries, keys, values, key_mask, log_rows, grad_rows = inputs
        scores = (
            jnp.einsum("qhd,khd->hqk", queries, keys, preferred_element_type=jnp.float32)
            * score_scale
        )
        scores = jnp.where(key_mask[None], scores, negative)
        probability = jnp.exp(scores - log_rows[..., None])
        grad_values = jnp.einsum(
            "hqk,qhd->khd",
            probability.astype(jnp.bfloat16),
            grad_rows,
            preferred_element_type=jnp.float32,
        )
        grad_prob = jnp.einsum(
            "qhd,khd->hqk", grad_rows, values, preferred_element_type=jnp.float32
        )
        row_delta = jnp.sum(grad_prob * probability, axis=-1, keepdims=True)
        grad_scores = (probability * (grad_prob - row_delta)).astype(jnp.bfloat16)
        grad_queries = (
            jnp.einsum("hqk,khd->qhd", grad_scores, keys, preferred_element_type=jnp.float32)
            * score_scale
        )
        grad_keys = (
            jnp.einsum("hqk,qhd->khd", grad_scores, queries, preferred_element_type=jnp.float32)
            * score_scale
        )
        return (
            grad_queries,
            grad_keys.reshape(slot_rows, width),
            grad_values.reshape(slot_rows, width),
        )

    grad_query_rot, grad_key_part, grad_value_part = lax.map(
        attend_back, (query_rot, all_keys, all_values, allowed, log_total, grad_attended)
    )
    grad_key_rot, grad_value = (
        lax.psum_scatter(
            grad_key_part.astype(jnp.bfloat16), "seq", scatter_dimension=1, tiled=True
        ).astype(jnp.float32),
        lax.psum_scatter(
            grad_value_part.astype(jnp.bfloat16), "seq", scatter_dimension=1, tiled=True
        ).astype(jnp.float32),
    )
    grad_query = turn_back(grad_query_rot)[0].reshape(slot_count, own_rows, width)
    grad_key = turn_back(grad_key_rot.reshape(four_dims))[0].reshape(slot_count, own_rows, width)
    gradient_query_key_value = jnp.concatenate([grad_query, grad_key, grad_value], axis=-1).astype(
        jnp.bfloat16
    )
    triple_weight_grad = jnp.einsum(
        "cqe,cqr->er",
        first_normed_tokens,
        gradient_query_key_value,
        preferred_element_type=jnp.float32,
    )
    grad_normed_one = jnp.einsum(
        "yma,ja->ymj",
        gradient_query_key_value,
        query_key_value_weight,
        preferred_element_type=jnp.float32,
    )
    first_back = jax.vjp(norm_modulate, residual, first_gain, shift_attn, scale_attn)[1]
    grad_residual, first_gain_grad, grad_shift_attn, grad_scale_attn = first_back(grad_normed_one)
    input_grad = (grad_middle + grad_residual).astype(jnp.bfloat16)
    grad_tokens = jnp.concatenate(
        [
            grad_shift_attn,
            grad_scale_attn,
            grad_gate_attn,
            grad_shift_mlp,
            grad_scale_mlp,
            grad_gate_mlp,
        ],
        axis=-1,
    )
    grad_modulation = jnp.einsum(
        "slm,slf->smf",
        own_member,
        grad_tokens,
        precision=highest,
        preferred_element_type=jnp.float32,
    )
    modulation_weight_grad = jnp.einsum(
        "smc,smf->cf",
        condition.astype(jnp.float32),
        grad_modulation,
        precision=highest,
        preferred_element_type=jnp.float32,
    )
    modulation_bias_grad = jnp.sum(grad_modulation, axis=(0, 1))
    vectors = [
        first_gain_grad,
        modulation_bias_grad,
        second_gain_grad,
        expand_bias_grad,
        reduce_bias_grad,
        stat_terms,
    ]
    flat_small = jnp.concatenate(vectors)
    summed_small = lax.psum(flat_small, ("dp", "seq"))
    small_results = []
    cursor = 0
    for vector in vectors:
        small_results.append(summed_small[cursor : cursor + vector.shape[0]])
        cursor = cursor + vector.shape[0]
    seq_count = lax.axis_size("seq")
    data_count = lax.axis_size("dp")
    matrix_parts = (
        lax.psum_scatter(
            block_order(modulation_weight_grad, seq_count, data_count),
            ("dp", "seq"),
            scatter_dimension=0,
            tiled=True,
        ),
        lax.psum_scatter(
            block_order(triple_weight_grad, seq_count, data_count),
            ("dp", "seq"),
            scatter_dimension=0,
            tiled=True,
        ),
        lax.psum_scatter(
            block_order(output_weight_grad, seq_count, data_count),
            ("dp", "seq"),
            scatter_dimension=0,
            tiled=True,
        ),
        lax.psum_scatter(
            block_order(expand_weight_grad, seq_count, data_count),
            ("dp", "seq"),
            scatter_dimension=0,
            tiled=True,
        ),
        lax.psum_scatter(
            block_order(reduce_weight_grad, seq_count, data_count),
            ("dp", "seq"),
            scatter_dimension=0,
            tiled=True,
        ),
    )
    totals = small_results[5]
    masked_rms = jnp.sqrt(totals[:3] / (totals[3] * width))
    return (
        block_out,
        input_grad,
        small_results[0],
        matrix_parts[0],
        small_results[1],
        matrix_parts[1],
        matrix_parts[2],
        small_results[2],
        matrix_parts[3],
        small_results[3],
        matrix_parts[4],
        small_results[4],
        masked_rms,
    )


def solution(mesh):
    in_specs = (
        P("dp", "seq", None),
        P("dp", None),
        P("dp", None),
        P("dp", None),
        P(),
        P(),
        P(),
        P(),
        P(),
        P(),
        P(),
        P(),
        P(),
        P(),
        P("dp", "seq", None),
    )
    out_specs = (
        P("dp", "seq", None),
        P("dp", "seq", None),
        P(),
        P("seq", "dp"),
        P(),
        P("seq", "dp"),
        P("seq", "dp"),
        P(),
        P("seq", "dp"),
        P(),
        P("seq", "dp"),
        P(),
        P(),
    )
    return jax.shard_map(local, mesh=mesh, in_specs=in_specs, out_specs=out_specs, check_vma=False)
```

profile of v0, /device:TPU:0, one launch (start us, length us, event | category | flops | bytes accessed | tf_op | source)
XLA Modules:
  0.0 905.5 jit_solution(2485126166303341673)
XLA Ops:
  26.8 3.1 copy.74
  32.1 3.0 copy.71
  36.2 6.6 multiply_add_fusion.2
  50.2 3.0 copy.72
  56.2 3.0 copy.73
  59.2 5.1 add_convert_fusion.1
  64.3 2.4 split.98
  68.1 3.1 copy.69
  75.4 18.9 %all-gather.5.cloned.1.call-done = bf16[1,1024,768]{2,1,0:T(8,128)(2,1)} async-done(((bf16[1,512,768]{2,1,0:T(8,128)(2,1)}), bf16[1,1024,768]{2,1,0:T(8,128)(2,1)}) %all-gather.5.cloned.1.call-update) | async-done | bytes 1572880 | tf_op jit(solution)/shard_map/all_gather | solution.py:135
  94.4 2.7 copy.75
  97.0 14.8 %fusion.8 = (f32[12,512]{1,0:T(8,128)S(1)}, f32[12,512,1024]{2,1,0:T(8,128)}) fusion(pred[512,1024]{1,0:T(8,128)(4,1)} %compare_and_fusion, bf16[512,12,64]{0,2,1:T(8,128)(2,1)} %fusion.57, bf16[1024,12,64]{0,2,1:T(8,128)(2,1)} %bitcast.275), kind=kOutput, calls=%fused_computation.20 | convolution fusion | flops 824174592 | bytes 28073984 | tf_op jit(solution)/shard_map/while/body/eval_jaxpr/qhd,khd->hqk/dot_general | solution.py:144
  111.8 11.8 %fusion = f32[12,512]{1,0:T(8,128)S(1)} fusion(f32[12,512]{1,0:T(8,128)S(1)} %get-tuple-element.132, f32[12,512,1024]{2,1,0:T(8,128)} %get-tuple-element.133, pred[512,1024]{1,0:T(8,128)(4,1)S(1)} %copy-done.15), kind=kLoop, calls=%fused_computation.6 | loop fusion | flops 25159680 | bytes 25739264 | tf_op jit(solution)/shard_map/while/body/eval_jaxpr/reduce_sum | solution.py:150
  124.9 2.6 copy.68
  127.5 13.2 %fusion.64 = bf16[12,64,512]{2,1,0:T(8,128)(2,1)S(1)} fusion(bf16[1024,12,64]{0,2,1:T(8,128)(2,1)} %bitcast.280, f32[12,512]{1,0:T(8,128)} %copy-done.39, f32[12,512]{1,0:T(8,128)} %copy-done.38, f32[12,512,1024]{2,1,0:T(8,128)} %get-tuple-element.133, pred[512,1024]{1,0:T(8,128)(4,1)} %compare_and_fusion), kind=kOutput, calls=%fused_computation.130 | convolution fusion | flops 837156864 | bytes 28098560 | tf_op jit(solution)/shard_map/while/body/eval_jaxpr/hqk,khd->qhd/dot_general | solution.py:152
  140.8 2.7 fusion.102
  145.2 2.6 fusion.69
  148.0 5.1 fusion.30
  153.1 12.1 %convert_reduce_fusion = (f32[3072]{0:T(1024)}, bf16[512,3072]{1,0:T(8,128)(2,1)}, f32[512,3072]{1,0:T(8,128)}) fusion(f32[512,3072]{1,0:T(8,128)S(1)} %fusion.69, f32[3072]{0:T(1024)S(1)} %copy-done.59, bf16[3072,768]{1,0:T(8,128)(2,1)} %param.27, bf16[1,512,768]{2,1,0:T(8,128)(2,1)S(1)} %get-tuple-element.85), kind=kOutput, calls=%fused_computation.46 | convolution fusion | flops 2458383360 | bytes 21258240 | tf_op jit(solution)/shard_map/kav,cv->kac/dot_general | solution.py:205
  165.2 7.6 multiply_reduce_fusion.1
  180.0 18.8 %multiply_reduce_fusion = (f32[12,512]{1,0:T(8,128)}, f32[12,512,1024]{2,1,0:T(8,128)}) fusion(f32[12,512]{1,0:T(8,128)} %log_add_fusion, f32[12,512,1024]{2,1,0:T(8,128)} %get-tuple-element.133, pred[512,1024]{1,0:T(8,128)(4,1)} %compare_and_fusion, bf16[512,12,64]{0,2,1:T(8,128)(2,1)} %bitcast.302, bf16[1024,12,64]{0,2,1:T(8,128)(2,1)} %bitcast.281), kind=kOutput, calls=%fused_computation.1 | convolution fusion | flops 836757504 | bytes 53264384 | tf_op jit(solution)/shard_map/while/body/eval_jaxpr/qhd,khd->hqk/dot_general | solution.py:254
  198.8 17.6 %multiply_convert_fusion = bf16[12,512,1024]{2,1,0:T(8,128)(2,1)S(1)} fusion(f32[12,512,1024]{2,1,0:T(8,128)} %get-tuple-element.138, f32[12,512]{1,0:T(8,128)} %get-tuple-element.137, f32[12,512]{1,0:T(8,128)} %log_add_fusion, f32[12,512,1024]{2,1,0:T(8,128)} %get-tuple-element.133, pred[512,1024]{1,0:T(8,128)(4,1)} %compare_and_fusion), kind=kLoop, calls=%fused_computation | loop fusion | flops 37748736 | bytes 63488000 | tf_op jit(solution)/shard_map/while/body/eval_jaxpr/convert_element_type | solution.py:258
  216.4 4.1 multiply_convert_fusion.2
  221.5 13.7 %fusion.38 = bf16[12,64,1024]{2,1,0:T(8,128)(2,1)} fusion(bf16[512,12,64]{0,2,1:T(8,128)(2,1)} %bitcast.303, f32[12,512]{1,0:T(8,128)} %log_add_fusion, f32[12,512,1024]{2,1,0:T(8,128)} %get-tuple-element.133, pred[512,1024]{1,0:T(8,128)(4,1)} %compare_and_fusion), kind=kOutput, calls=%fused_computation.77 | convolution fusion | flops 831258624 | bytes 28073984 | tf_op jit(solution)/shard_map/while/body/eval_jaxpr/hqk,qhd->khd/dot_general | solution.py:248
  242.5 3.3 copy.83
  245.7 4.4 reshape.1485
  250.1 9.0 fusion.107
  262.0 3.2 fusion.59
  268.0 8.4 reduce-scatter.10.cloned.1.call-done
  276.3 3.7 bitcast_dynamic-update-slice_fusion
  289.9 4.4 fusion.106
  302.7 11.0 %multiply_convert_fusion.1 = (bf16[3072,512]{0,1:T(8,128)(2,1)}, bf16[3072,512]{0,1:T(8,128)(2,1)}) fusion(f32[512,3072]{1,0:T(8,128)} %copy-done.8, f32[3072]{0:T(1024)S(1)} %copy-done.60, f32[512,3072]{1,0:T(8,128)} %get-tuple-element.135), kind=kLoop, calls=%fused_computation.45 | loop fusion | flops 42467328 | bytes 18886656 | tf_op jit(solution)/shard_map/convert_element_type | solution.py:179
  313.6 4.8 copy.84
  318.4 4.8 convolution_bitcast_fusion.2
  323.2 12.7 %copy.86 = f32[16,2,384,192]{2,1,0,3:T(2,128)} copy(f32[16,2,384,192]{2,3,0,1:T(8,128)S(1)} %convolution_bitcast_fusion.2) | data formatting | bytes 18874368 | tf_op jit(solution)/shard_map/transpose | solution.py:64
  336.0 12.5 %reshape.1486 = f32[12288,192]{0,1:T(8,128)} reshape(f32[16,2,384,192]{2,1,0,3:T(2,128)} %copy.86) | data formatting | bytes 18874368 | tf_op jit(solution)/shard_map/reshape | solution.py:65
  350.9 4.8 copy.99
  355.7 4.7 convolution_bitcast_fusion
  360.5 11.1 %copy.89 = f32[16,2,1536,48]{2,1,0,3:T(2,128)} copy(f32[16,2,1536,48]{2,3,0,1:T(8,128)S(1)} %convolution_bitcast_fusion) | data formatting | bytes 18874368 | tf_op jit(solution)/shard_map/transpose | solution.py:64
  371.6 12.2 %reshape.1487 = f32[49152,48]{0,1:T(8,128)} reshape(f32[16,2,1536,48]{2,1,0,3:T(2,128)} %copy.89) | data formatting | bytes 18874368 | tf_op jit(solution)/shard_map/reshape | solution.py:65
  388.1 4.5 convolution_bitcast_fusion.3
  392.5 11.4 %copy.81 = f32[16,2,384,144]{2,1,0,3:T(2,128)} copy(f32[16,2,384,144]{2,3,0,1:T(8,128)} %convolution_bitcast_fusion.3) | data formatting | bytes 14155776 | tf_op jit(solution)/shard_map/transpose | solution.py:64
  403.9 9.8 %reshape.1484 = f32[12288,144]{0,1:T(8,128)} reshape(f32[16,2,384,144]{2,1,0,3:T(2,128)} %copy.81) | data formatting | bytes 14155776 | tf_op jit(solution)/shard_map/reshape | solution.py:65
  414.5 3.9 concatenate.72
  418.4 40.4 %psum.7 = f32[9988]{0:T(1024)} all-reduce(f32[9988]{0:T(1024)} %concatenate.72), channel_id=1, replica_groups=mesh['dp'=16,'seq'=2] {'dp','seq'}, use_global_device_ids=true, to_apply=%region_26.27 | all-reduce | flops 9988 | bytes 79904 | tf_op jit(solution)/shard_map/psum | solution.py:339
  465.9 22.6 %reduce-scatter.12.cloned.1.call-done = f32[64,288]{1,0:T(8,128)} async-done(((f32[2048,288]{1,0:T(8,128)}), f32[64,288]{1,0:T(8,128)}) %reduce-scatter.12.cloned.1.call-update) | async-done | bytes 73744 | tf_op jit(solution)/shard_map/reduce_scatter | solution.py:348
  488.5 141.9 %reduce-scatter.18.cloned.1.call-done = f32[384,192]{0,1:T(8,128)} async-done(((f32[12288,192]{0,1:T(8,128)}), f32[384,192]{0,1:T(8,128)}) %reduce-scatter.18.cloned.1.call-update) | async-done | bytes 294928 | tf_op jit(solution)/shard_map/reduce_scatter | solution.py:366
  630.4 143.0 %reduce-scatter.20.cloned.1.call-done = f32[1536,48]{0,1:T(8,128)} async-done(((f32[49152,48]{0,1:T(8,128)}), f32[1536,48]{0,1:T(8,128)}) %reduce-scatter.20.cloned.1.call-update) | async-done | bytes 294928 | tf_op jit(solution)/shard_map/reduce_scatter | solution.py:372
  773.4 125.4 %reduce-scatter.14.cloned.1.call-done = f32[384,144]{0,1:T(8,128)} async-done(((f32[12288,144]{0,1:T(8,128)}), f32[384,144]{0,1:T(8,128)}) %reduce-scatter.14.cloned.1.call-update) | async-done | bytes 221200 | tf_op jit(solution)/shard_map/reduce_scatter | solution.py:354
  (243 shorter events, 94.7 us)
Async XLA Ops:
  7.2 36.2 %copy-start = (bf16[768,2304]{1,0:T(8,128)(2,1)S(1)}, bf16[768,2304]{1,0:T(8,128)(2,1)}, u32[]{:S(2)}) copy-start(bf16[768,2304]{1,0:T(8,128)(2,1)} %param.22) | copy-start | bytes 10616836
  7.2 87.2 %all-gather.5.cloned.1.call-start = ((), (), s32[]{:S(2)}) async-start(), calls=%async_computation.8 | async-start | bytes 2359296 | tf_op jit(solution)/shard_map/all_gather | solution.py:135
  11.4 31.4 %copy-start.41 = (f32[512]{0:T(512)}, f32[512]{0:T(512)S(1)}, u32[]{:S(2)}) copy-start(f32[512]{0:T(512)S(1)} %broadcast_multiply_fusion.4) | copy-start | bytes 6148
  13.5 29.3 %copy-start.45 = (f32[512]{0:T(512)}, f32[512]{0:T(512)S(1)}, u32[]{:S(2)}) copy-start(f32[512]{0:T(512)S(1)} %fusion.84) | copy-start | bytes 6148
  18.6 3.2 copy-start.51
  36.2 6.6 copy-start.5
  36.2 6.6 copy-start.43
  42.9 3.6 copy-start.2
  43.4 3.3 copy-start.23
  64.3 3.3 copy-start.48
  64.3 60.6 %all-gather.3.cloned.1.call-start = ((), (), s32[]{:S(2)}) async-start(), calls=%async_computation.7 | async-start | bytes 2359296 | tf_op jit(solution)/shard_map/all_gather | solution.py:136
  66.7 198.4 %reduce-scatter.8.cloned.1.call-start = ((), (), s32[]{:S(2)}) async-start(), calls=%async_computation.9 | async-start | bytes 2359296 | tf_op jit(solution)/shard_map/reduce_scatter | solution.py:277
  68.1 4.7 copy-start.61
  68.1 4.7 copy-start.62
  97.0 14.8 %copy-start.15 = (pred[512,1024]{1,0:T(8,128)(4,1)S(1)}, pred[512,1024]{1,0:T(8,128)(4,1)}, u32[]{:S(2)}) copy-start(pred[512,1024]{1,0:T(8,128)(4,1)} %compare_and_fusion) | copy-start | bytes 1572868
  111.8 11.8 %copy-start.38 = (f32[12,512]{1,0:T(8,128)}, f32[12,512]{1,0:T(8,128)S(1)}, u32[]{:S(2)}) copy-start(f32[12,512]{1,0:T(8,128)S(1)} %get-tuple-element.132) | copy-start | bytes 73732
  127.5 16.3 %slice-start = ((s8[9437184]{0:T(1024)(128)(4,1)}), s8[4194304]{0:T(1024)(128)(4,1)S(1)}, s32[]{:S(2)}) async-start(s8[9437184]{0:T(1024)(128)(4,1)} %bitcast.271), calls=%async_computation.16 | async-start | bytes 8388608
  127.5 13.2 %copy-start.6 = (bf16[1,512,768]{2,1,0:T(8,128)(2,1)S(1)}, bf16[1,512,768]{2,1,0:T(8,128)(2,1)}, u32[]{:S(2)}) copy-start(bf16[1,512,768]{2,1,0:T(8,128)(2,1)} %param.15) | copy-start | bytes 2359300
  127.5 13.2 %copy-start.34 = (bf16[768,768]{1,0:T(8,128)(2,1)S(1)}, bf16[768,768]{1,0:T(8,128)(2,1)}, u32[]{:S(2)}) copy-start(bf16[768,768]{1,0:T(8,128)(2,1)} %param.23) | copy-start | bytes 3538948
  127.5 16.3 %slice-start.1 = ((s8[9437184]{0:T(1024)(128)(4,1)}), s8[4194304]{0:T(1024)(128)(4,1)S(1)}, s32[]{:S(2)}) async-start(s8[9437184]{0:T(1024)(128)(4,1)} %bitcast.271), calls=%async_computation.17 | async-start | bytes 8388608
  127.5 16.3 %slice-start.2 = ((s8[9437184]{0:T(1024)(128)(4,1)}), s8[1048576]{0:T(1024)(128)(4,1)S(1)}, s32[]{:S(2)}) async-start(s8[9437184]{0:T(1024)(128)(4,1)} %bitcast.271), calls=%async_computation.18 | async-start | bytes 2097152
  140.7 3.1 copy-start.16
  140.7 3.1 copy-start.47
  140.7 4.4 slice-start.3
  143.4 21.8 %copy-start.21 = (f32[512,768]{1,0:T(8,128)}, f32[512,768]{1,0:T(8,128)S(1)}, u32[]{:S(2)}) copy-start(f32[512,768]{1,0:T(8,128)S(1)} %get-tuple-element.134) | copy-start | bytes 4718596
  143.4 29.3 %copy-start.3 = (f32[1,512,768]{2,1,0:T(8,128)}, f32[1,512,768]{2,1,0:T(8,128)S(1)}, u32[]{:S(2)}) copy-start(f32[1,512,768]{2,1,0:T(8,128)S(1)} %get-tuple-element.94) | copy-start | bytes 4718596
  143.8 4.0 slice-start.5
  145.1 8.0 copy-start.24
  148.0 5.1 copy-start.8
  153.1 12.1 %copy-start.64 = (f32[768]{0:T(1024)S(1)}, f32[768]{0:T(1024)}, u32[]{:S(2)}) copy-start(f32[768]{0:T(1024)} %param.28) | copy-start | bytes 9220
  198.8 17.6 %copy-start.18 = (bf16[512,12,64]{0,2,1:T(8,128)(2,1)S(1)}, bf16[512,12,64]{0,2,1:T(8,128)(2,1)}, u32[]{:S(2)}) copy-start(bf16[512,12,64]{0,2,1:T(8,128)(2,1)} %fusion.57) | copy-start | bytes 2359300
  216.4 5.1 copy-start.1
  221.5 54.8 %reduce-scatter.10.cloned.1.call-start = ((), (), s32[]{:S(2)}) async-start(), calls=%async_computation.10 | async-start | bytes 2359296 | tf_op jit(solution)/shard_map/reduce_scatter | solution.py:280
  235.3 230.6 %reduce-scatter.16.cloned.1.call-start = ((), (), s32[]{:S(2)}) async-start(), calls=%async_computation.13 | async-start | bytes 2433024 | tf_op jit(solution)/shard_map/reduce_scatter | solution.py:360
  250.1 10.3 %copy-start.37 = (f32[512,64]{0,1:T(8,128)S(1)}, f32[512,64]{0,1:T(8,128)}, u32[]{:S(2)}) copy-start(f32[512,64]{0,1:T(8,128)} %get-tuple-element.114) | copy-start | bytes 393220
  261.9 226.6 %reduce-scatter.12.cloned.1.call-start = ((), (), s32[]{:S(2)}) async-start(), calls=%async_computation.11 | async-start | bytes 3244032 | tf_op jit(solution)/shard_map/reduce_scatter | solution.py:348
  276.3 3.7 copy-start.7
  276.3 3.7 copy-start.42
  276.3 3.8 copy-start.44
  276.3 3.8 copy-start.46
  280.1 3.8 copy-start.13
  280.1 3.8 copy-start.17
  280.1 3.8 copy-start.22
  280.1 3.8 copy-start.55
  289.9 6.1 copy-start.58
  300.3 330.1 %reduce-scatter.18.cloned.1.call-start = ((), (), s32[]{:S(2)}) async-start(), calls=%async_computation.14 | async-start | bytes 9732096 | tf_op jit(solution)/shard_map/reduce_scatter | solution.py:366
  348.5 424.8 %reduce-scatter.20.cloned.1.call-start = ((), (), s32[]{:S(2)}) async-start(), calls=%async_computation.15 | async-start | bytes 9732096 | tf_op jit(solution)/shard_map/reduce_scatter | solution.py:372
  383.8 514.9 %reduce-scatter.14.cloned.1.call-start = ((), (), s32[]{:S(2)}) async-start(), calls=%async_computation.12 | async-start | bytes 7299072 | tf_op jit(solution)/shard_map/reduce_scatter | solution.py:354
  (34 other events, 57.7 us)
Sparse Core Ops, SparseCore 0:
  64.4 29.8 all-gather.4
  96.5 27.2 all-gather.2
  221.6 26.3 reduce-scatter.7
  250.2 26.0 reduce-scatter.9
  282.0 99.0 reduce-scatter.15
  387.9 100.5 reduce-scatter.11
  496.0 134.3 reduce-scatter.17
  636.9 136.4 reduce-scatter.19
  780.6 118.1 reduce-scatter.13
where the time goes:
time: 914 us; the launch traced here: 906 us
  waiting for transfers between devices  460 us (50%)
  local copies, waits for them, and re-layouts  157 us (17%)
  matrix products  136 us (15%)
  other arithmetic  96.3 us (11%)
  blocking collectives  40.4 us (4%)
  between operations  15.5 us (2%)
    reduce_scatter x1, waiting for transfers between devices, local(): lax.psum_scatter(block_order(reduce_weight_grad, seq_count, data_count),...  143 us
    reduce_scatter x1, waiting for transfers between devices, local(): lax.psum_scatter(block_order(expand_weight_grad, seq_count, data_count),...  142 us
    reduce_scatter x1, waiting for transfers between devices, local(): lax.psum_scatter(block_order(triple_weight_grad, seq_count, data_count),...  125 us
    psum x1, blocking collectives, local(): summed_small = lax.psum(flat_small, ('dp', 'seq'))  40.4 us
    transpose x5, local copies, waits for them, and re-layouts, block_order(): arranged = arranged.transpose(2, 0, 1, 3)  40.4 us
    reshape x4, local copies, waits for them, and re-layouts, block_order(): return arranged.reshape(data_count * rows, cols // data_count)  39 us
    reduce_scatter x1, waiting for transfers between devices, local(): lax.psum_scatter(block_order(modulation_weight_grad, seq_count, data_coun...  22.6 us
    all_gather x1, waiting for transfers between devices, local(): lax.all_gather(key_rot, 'seq', axis=1, tiled=True)  18.9 us
  transfers between devices with their start and end apart: 9, of which 6 were waited for; matrix products, arithmetic and copies ran while one was open for 25% of the time, Pallas kernels for 0%

commit v1 on v0

--- a/solution.py
+++ b/solution.py
@@ -336,7 +336,9 @@
         stat_terms,
     ]
     flat_small = jnp.concatenate(vectors)
-    summed_small = lax.psum(flat_small, ("dp", "seq"))
+    summed_small = flat_small
+    for pp in ("seq", "dp"):
+        summed_small = jax.lax.psum(summed_small, axis_name=pp)
     small_results = []
     cursor = 0
     for vector in vectors:

time: 914 us -> 914 us (level)
  blocking collectives: 40.4 us -> 69.4 us
  waiting for transfers between devices: 460 us -> 432 us
    psum x1 -> x2, blocking collectives: 40.4 us -> 69.4 us  [local(): summed_small = jax.lax.psum(summed_small, axis_name=pp)]
    reduce_scatter x1, waiting for transfers between devices: 22.6 us -> 0.01 us  [local(): lax.psum_scatter(block_order(modulation_weight_grad, seq_count, data_coun...]
  transfers between devices with their start and end apart: 9 -> 9, of which waited for: 6 -> 5; matrix products, arithmetic and copies ran while one was open for 25% -> 25% of each run, Pallas kernels for 0% -> 0%
where the time goes in v1:
time: 914 us; the launch traced here: 905 us
  waiting for transfers between devices  432 us (47%)
  local copies, waits for them, and re-layouts  157 us (17%)
  matrix products  135 us (15%)
  other arithmetic  96.3 us (11%)
  blocking collectives  69.4 us (8%)
  between operations  15.5 us (2%)
    reduce_scatter x1, waiting for transfers between devices, local(): lax.psum_scatter(block_order(reduce_weight_grad, seq_count, data_count),...  143 us
    reduce_scatter x1, waiting for transfers between devices, local(): lax.psum_scatter(block_order(expand_weight_grad, seq_count, data_count),...  136 us
    reduce_scatter x1, waiting for transfers between devices, local(): lax.psum_scatter(block_order(triple_weight_grad, seq_count, data_count),...  125 us
    psum x2, blocking collectives, local(): summed_small = jax.lax.psum(summed_small, axis_name=pp)  69.4 us
    transpose x5, local copies, waits for them, and re-layouts, block_order(): arranged = arranged.transpose(2, 0, 1, 3)  40.4 us
    reshape x4, local copies, waits for them, and re-layouts, block_order(): return arranged.reshape(data_count * rows, cols // data_count)  38.9 us
    all_gather x1, waiting for transfers between devices, local(): lax.all_gather(key_rot, 'seq', axis=1, tiled=True)  18.9 us
    dot_general x1, matrix products, attend_back(): jnp.einsum('qhd,khd->hqk', grad_rows, values, preferred_element_type=jnp....  18.8 us
  transfers between devices with their start and end apart: 9, of which 5 were waited for; matrix products, arithmetic and copies ran while one was open for 25% of the time, Pallas kernels for 0%

profile of v1, /device:TPU:0, one launch (start us, length us, event | category | flops | bytes accessed | tf_op | source)
XLA Modules:
  0.0 905.4 jit_solution(8465253501353433925)
XLA Ops:
  26.7 3.0 copy.74
  32.0 3.0 copy.71
  36.2 6.6 multiply_add_fusion.2
  50.1 3.0 copy.72
  56.1 3.1 copy.73
  59.2 5.1 add_convert_fusion.1
  64.3 2.4 split.98
  68.1 3.1 copy.69
  75.4 18.9 %all-gather.5.cloned.1.call-done = bf16[1,1024,768]{2,1,0:T(8,128)(2,1)} async-done(((bf16[1,512,768]{2,1,0:T(8,128)(2,1)}), bf16[1,1024,768]{2,1,0:T(8,128)(2,1)}) %all-gather.5.cloned.1.call-update) | async-done | bytes 1572880 | tf_op jit(solution)/shard_map/all_gather | solution.py:135
  94.3 2.7 copy.75
  97.0 14.8 %fusion.8 = (f32[12,512]{1,0:T(8,128)S(1)}, f32[12,512,1024]{2,1,0:T(8,128)}) fusion(pred[512,1024]{1,0:T(8,128)(4,1)} %compare_and_fusion, bf16[512,12,64]{0,2,1:T(8,128)(2,1)} %fusion.57, bf16[1024,12,64]{0,2,1:T(8,128)(2,1)} %bitcast.275), kind=kOutput, calls=%fused_computation.20 | convolution fusion | flops 824174592 | bytes 28073984 | tf_op jit(solution)/shard_map/while/body/eval_jaxpr/qhd,khd->hqk/dot_general | solution.py:144
  111.8 11.8 %fusion = f32[12,512]{1,0:T(8,128)S(1)} fusion(f32[12,512]{1,0:T(8,128)S(1)} %get-tuple-element.132, f32[12,512,1024]{2,1,0:T(8,128)} %get-tuple-element.133, pred[512,1024]{1,0:T(8,128)(4,1)S(1)} %copy-done.15), kind=kLoop, calls=%fused_computation.6 | loop fusion | flops 25159680 | bytes 25739264 | tf_op jit(solution)/shard_map/while/body/eval_jaxpr/reduce_sum | solution.py:150
  124.8 2.6 copy.68
  127.4 13.2 %fusion.64 = bf16[12,64,512]{2,1,0:T(8,128)(2,1)S(1)} fusion(bf16[1024,12,64]{0,2,1:T(8,128)(2,1)} %bitcast.280, f32[12,512]{1,0:T(8,128)} %copy-done.39, f32[12,512]{1,0:T(8,128)} %copy-done.38, f32[12,512,1024]{2,1,0:T(8,128)} %get-tuple-element.133, pred[512,1024]{1,0:T(8,128)(4,1)} %compare_and_fusion), kind=kOutput, calls=%fused_computation.130 | convolution fusion | flops 837156864 | bytes 28098560 | tf_op jit(solution)/shard_map/while/body/eval_jaxpr/hqk,khd->qhd/dot_general | solution.py:152
  140.7 2.7 fusion.102
  145.1 2.6 fusion.69
  147.9 5.1 fusion.30
  153.0 12.1 %convert_reduce_fusion = (f32[3072]{0:T(1024)}, bf16[512,3072]{1,0:T(8,128)(2,1)}, f32[512,3072]{1,0:T(8,128)}) fusion(f32[512,3072]{1,0:T(8,128)S(1)} %fusion.69, f32[3072]{0:T(1024)S(1)} %copy-done.59, bf16[3072,768]{1,0:T(8,128)(2,1)} %param.27, bf16[1,512,768]{2,1,0:T(8,128)(2,1)S(1)} %get-tuple-element.85), kind=kOutput, calls=%fused_computation.46 | convolution fusion | flops 2458383360 | bytes 21258240 | tf_op jit(solution)/shard_map/kav,cv->kac/dot_general | solution.py:205
  165.1 7.5 multiply_reduce_fusion.1
  179.9 18.8 %multiply_reduce_fusion = (f32[12,512]{1,0:T(8,128)}, f32[12,512,1024]{2,1,0:T(8,128)}) fusion(f32[12,512]{1,0:T(8,128)} %log_add_fusion, f32[12,512,1024]{2,1,0:T(8,128)} %get-tuple-element.133, pred[512,1024]{1,0:T(8,128)(4,1)} %compare_and_fusion, bf16[512,12,64]{0,2,1:T(8,128)(2,1)} %bitcast.302, bf16[1024,12,64]{0,2,1:T(8,128)(2,1)} %bitcast.281), kind=kOutput, calls=%fused_computation.1 | convolution fusion | flops 836757504 | bytes 53264384 | tf_op jit(solution)/shard_map/while/body/eval_jaxpr/qhd,khd->hqk/dot_general | solution.py:254
  198.7 17.6 %multiply_convert_fusion = bf16[12,512,1024]{2,1,0:T(8,128)(2,1)S(1)} fusion(f32[12,512,1024]{2,1,0:T(8,128)} %get-tuple-element.138, f32[12,512]{1,0:T(8,128)} %get-tuple-element.137, f32[12,512]{1,0:T(8,128)} %log_add_fusion, f32[12,512,1024]{2,1,0:T(8,128)} %get-tuple-element.133, pred[512,1024]{1,0:T(8,128)(4,1)} %compare_and_fusion), kind=kLoop, calls=%fused_computation | loop fusion | flops 37748736 | bytes 63488000 | tf_op jit(solution)/shard_map/while/body/eval_jaxpr/convert_element_type | solution.py:258
  216.3 4.1 multiply_convert_fusion.2
  221.4 13.7 %fusion.38 = bf16[12,64,1024]{2,1,0:T(8,128)(2,1)} fusion(bf16[512,12,64]{0,2,1:T(8,128)(2,1)} %bitcast.303, f32[12,512]{1,0:T(8,128)} %log_add_fusion, f32[12,512,1024]{2,1,0:T(8,128)} %get-tuple-element.133, pred[512,1024]{1,0:T(8,128)(4,1)} %compare_and_fusion), kind=kOutput, calls=%fused_computation.77 | convolution fusion | flops 831258624 | bytes 28073984 | tf_op jit(solution)/shard_map/while/body/eval_jaxpr/hqk,qhd->khd/dot_general | solution.py:248
  242.3 3.3 copy.83
  245.6 4.4 reshape.1485
  250.0 9.0 fusion.107
  261.8 3.2 fusion.59
  267.8 8.4 reduce-scatter.10.cloned.1.call-done
  276.2 3.7 bitcast_dynamic-update-slice_fusion
  289.8 4.4 fusion.106
  302.5 11.0 %multiply_convert_fusion.1 = (bf16[3072,512]{0,1:T(8,128)(2,1)}, bf16[3072,512]{0,1:T(8,128)(2,1)}) fusion(f32[512,3072]{1,0:T(8,128)} %copy-done.8, f32[3072]{0:T(1024)S(1)} %copy-done.60, f32[512,3072]{1,0:T(8,128)} %get-tuple-element.135), kind=kLoop, calls=%fused_computation.45 | loop fusion | flops 42467328 | bytes 18886656 | tf_op jit(solution)/shard_map/convert_element_type | solution.py:179
  313.5 4.7 copy.84
  318.3 4.8 convolution_bitcast_fusion.2
  323.1 12.7 %copy.86 = f32[16,2,384,192]{2,1,0,3:T(2,128)} copy(f32[16,2,384,192]{2,3,0,1:T(8,128)S(1)} %convolution_bitcast_fusion.2) | data formatting | bytes 18874368 | tf_op jit(solution)/shard_map/transpose | solution.py:64
  335.8 12.5 %reshape.1486 = f32[12288,192]{0,1:T(8,128)} reshape(f32[16,2,384,192]{2,1,0,3:T(2,128)} %copy.86) | data formatting | bytes 18874368 | tf_op jit(solution)/shard_map/reshape | solution.py:65
  350.8 4.8 copy.99
  355.6 4.7 convolution_bitcast_fusion
  360.3 11.1 %copy.89 = f32[16,2,1536,48]{2,1,0,3:T(2,128)} copy(f32[16,2,1536,48]{2,3,0,1:T(8,128)S(1)} %convolution_bitcast_fusion) | data formatting | bytes 18874368 | tf_op jit(solution)/shard_map/transpose | solution.py:64
  371.4 12.2 %reshape.1487 = f32[49152,48]{0,1:T(8,128)} reshape(f32[16,2,1536,48]{2,1,0,3:T(2,128)} %copy.89) | data formatting | bytes 18874368 | tf_op jit(solution)/shard_map/reshape | solution.py:65
  387.9 4.3 convolution_bitcast_fusion.3
  392.2 11.4 %copy.81 = f32[16,2,384,144]{2,1,0,3:T(2,128)} copy(f32[16,2,384,144]{2,3,0,1:T(8,128)} %convolution_bitcast_fusion.3) | data formatting | bytes 14155776 | tf_op jit(solution)/shard_map/transpose | solution.py:64
  403.6 9.8 %reshape.1484 = f32[12288,144]{0,1:T(8,128)} reshape(f32[16,2,384,144]{2,1,0,3:T(2,128)} %copy.81) | data formatting | bytes 14155776 | tf_op jit(solution)/shard_map/reshape | solution.py:65
  414.2 3.8 concatenate.72
  418.0 8.5 psum.14
  426.5 60.9 %psum.15 = f32[9988]{0:T(1024)} all-reduce(f32[9988]{0:T(1024)} %psum.14), channel_id=1, replica_groups=mesh['dp'=16,'seq'=2] {'dp'}, use_global_device_ids=true, to_apply=%region_27.28 | all-reduce | flops 9988 | bytes 79904 | tf_op jit(solution)/shard_map/psum | solution.py:341
  494.5 136.1 %reduce-scatter.18.cloned.1.call-done = f32[384,192]{0,1:T(8,128)} async-done(((f32[12288,192]{0,1:T(8,128)}), f32[384,192]{0,1:T(8,128)}) %reduce-scatter.18.cloned.1.call-update) | async-done | bytes 294928 | tf_op jit(solution)/shard_map/reduce_scatter | solution.py:368
  630.6 142.8 %reduce-scatter.20.cloned.1.call-done = f32[1536,48]{0,1:T(8,128)} async-done(((f32[49152,48]{0,1:T(8,128)}), f32[1536,48]{0,1:T(8,128)}) %reduce-scatter.20.cloned.1.call-update) | async-done | bytes 294928 | tf_op jit(solution)/shard_map/reduce_scatter | solution.py:374
  773.4 125.3 %reduce-scatter.14.cloned.1.call-done = f32[384,144]{0,1:T(8,128)} async-done(((f32[12288,144]{0,1:T(8,128)}), f32[384,144]{0,1:T(8,128)}) %reduce-scatter.14.cloned.1.call-update) | async-done | bytes 221200 | tf_op jit(solution)/shard_map/reduce_scatter | solution.py:356
  (244 shorter events, 94.6 us)
Async XLA Ops:
  7.2 36.1 %copy-start = (bf16[768,2304]{1,0:T(8,128)(2,1)S(1)}, bf16[768,2304]{1,0:T(8,128)(2,1)}, u32[]{:S(2)}) copy-start(bf16[768,2304]{1,0:T(8,128)(2,1)} %param.22) | copy-start | bytes 10616836
  7.2 87.1 %all-gather.5.cloned.1.call-start = ((), (), s32[]{:S(2)}) async-start(), calls=%async_computation.8 | async-start | bytes 2359296 | tf_op jit(solution)/shard_map/all_gather | solution.py:135
  11.4 31.4 %copy-start.41 = (f32[512]{0:T(512)}, f32[512]{0:T(512)S(1)}, u32[]{:S(2)}) copy-start(f32[512]{0:T(512)S(1)} %broadcast_multiply_fusion.4) | copy-start | bytes 6148
  13.5 29.3 %copy-start.45 = (f32[512]{0:T(512)}, f32[512]{0:T(512)S(1)}, u32[]{:S(2)}) copy-start(f32[512]{0:T(512)S(1)} %fusion.84) | copy-start | bytes 6148
  18.6 3.1 copy-start.51
  36.2 6.6 copy-start.5
  36.2 6.6 copy-start.43
  42.8 3.6 copy-start.2
  43.3 3.3 copy-start.23
  64.2 3.3 copy-start.48
  64.2 60.6 %all-gather.3.cloned.1.call-start = ((), (), s32[]{:S(2)}) async-start(), calls=%async_computation.7 | async-start | bytes 2359296 | tf_op jit(solution)/shard_map/all_gather | solution.py:136
  66.7 198.3 %reduce-scatter.8.cloned.1.call-start = ((), (), s32[]{:S(2)}) async-start(), calls=%async_computation.9 | async-start | bytes 2359296 | tf_op jit(solution)/shard_map/reduce_scatter | solution.py:277
  68.1 4.7 copy-start.61
  68.1 4.7 copy-start.62
  97.0 14.8 %copy-start.15 = (pred[512,1024]{1,0:T(8,128)(4,1)S(1)}, pred[512,1024]{1,0:T(8,128)(4,1)}, u32[]{:S(2)}) copy-start(pred[512,1024]{1,0:T(8,128)(4,1)} %compare_and_fusion) | copy-start | bytes 1572868
  111.8 11.8 %copy-start.38 = (f32[12,512]{1,0:T(8,128)}, f32[12,512]{1,0:T(8,128)S(1)}, u32[]{:S(2)}) copy-start(f32[12,512]{1,0:T(8,128)S(1)} %get-tuple-element.132) | copy-start | bytes 73732
  127.4 16.3 %slice-start = ((s8[9437184]{0:T(1024)(128)(4,1)}), s8[4194304]{0:T(1024)(128)(4,1)S(1)}, s32[]{:S(2)}) async-start(s8[9437184]{0:T(1024)(128)(4,1)} %bitcast.271), calls=%async_computation.16 | async-start | bytes 8388608
  127.4 13.2 %copy-start.6 = (bf16[1,512,768]{2,1,0:T(8,128)(2,1)S(1)}, bf16[1,512,768]{2,1,0:T(8,128)(2,1)}, u32[]{:S(2)}) copy-start(bf16[1,512,768]{2,1,0:T(8,128)(2,1)} %param.15) | copy-start | bytes 2359300
  127.4 13.2 %copy-start.34 = (bf16[768,768]{1,0:T(8,128)(2,1)S(1)}, bf16[768,768]{1,0:T(8,128)(2,1)}, u32[]{:S(2)}) copy-start(bf16[768,768]{1,0:T(8,128)(2,1)} %param.23) | copy-start | bytes 3538948
  127.4 16.3 %slice-start.1 = ((s8[9437184]{0:T(1024)(128)(4,1)}), s8[4194304]{0:T(1024)(128)(4,1)S(1)}, s32[]{:S(2)}) async-start(s8[9437184]{0:T(1024)(128)(4,1)} %bitcast.271), calls=%async_computation.17 | async-start | bytes 8388608
  127.4 16.3 %slice-start.2 = ((s8[9437184]{0:T(1024)(128)(4,1)}), s8[1048576]{0:T(1024)(128)(4,1)S(1)}, s32[]{:S(2)}) async-start(s8[9437184]{0:T(1024)(128)(4,1)} %bitcast.271), calls=%async_computation.18 | async-start | bytes 2097152
  140.6 3.1 copy-start.16
  140.6 3.1 copy-start.47
  140.7 4.4 slice-start.3
  143.3 21.7 %copy-start.21 = (f32[512,768]{1,0:T(8,128)}, f32[512,768]{1,0:T(8,128)S(1)}, u32[]{:S(2)}) copy-start(f32[512,768]{1,0:T(8,128)S(1)} %get-tuple-element.134) | copy-start | bytes 4718596
  143.4 29.3 %copy-start.3 = (f32[1,512,768]{2,1,0:T(8,128)}, f32[1,512,768]{2,1,0:T(8,128)S(1)}, u32[]{:S(2)}) copy-start(f32[1,512,768]{2,1,0:T(8,128)S(1)} %get-tuple-element.94) | copy-start | bytes 4718596
  143.8 4.0 slice-start.5
  145.1 7.9 copy-start.24
  147.9 5.1 copy-start.8
  153.0 12.1 %copy-start.64 = (f32[768]{0:T(1024)S(1)}, f32[768]{0:T(1024)}, u32[]{:S(2)}) copy-start(f32[768]{0:T(1024)} %param.28) | copy-start | bytes 9220
  198.7 17.6 %copy-start.18 = (bf16[512,12,64]{0,2,1:T(8,128)(2,1)S(1)}, bf16[512,12,64]{0,2,1:T(8,128)(2,1)}, u32[]{:S(2)}) copy-start(bf16[512,12,64]{0,2,1:T(8,128)(2,1)} %fusion.57) | copy-start | bytes 2359300
  216.3 5.1 copy-start.1
  221.4 54.8 %reduce-scatter.10.cloned.1.call-start = ((), (), s32[]{:S(2)}) async-start(), calls=%async_computation.10 | async-start | bytes 2359296 | tf_op jit(solution)/shard_map/reduce_scatter | solution.py:280
  235.1 259.4 %reduce-scatter.16.cloned.1.call-start = ((), (), s32[]{:S(2)}) async-start(), calls=%async_computation.13 | async-start | bytes 2433024 | tf_op jit(solution)/shard_map/reduce_scatter | solution.py:362
  250.0 10.3 %copy-start.37 = (f32[512,64]{0,1:T(8,128)S(1)}, f32[512,64]{0,1:T(8,128)}, u32[]{:S(2)}) copy-start(f32[512,64]{0,1:T(8,128)} %get-tuple-element.114) | copy-start | bytes 393220
  261.8 232.7 %reduce-scatter.12.cloned.1.call-start = ((), (), s32[]{:S(2)}) async-start(), calls=%async_computation.11 | async-start | bytes 3244032 | tf_op jit(solution)/shard_map/reduce_scatter | solution.py:350
  276.2 3.7 copy-start.7
  276.2 3.7 copy-start.42
  276.2 3.8 copy-start.44
  276.2 3.8 copy-start.46
  280.0 3.8 copy-start.13
  280.0 3.8 copy-start.17
  280.0 3.8 copy-start.22
  280.0 3.8 copy-start.55
  289.8 6.1 copy-start.58
  300.1 330.5 %reduce-scatter.18.cloned.1.call-start = ((), (), s32[]{:S(2)}) async-start(), calls=%async_computation.14 | async-start | bytes 9732096 | tf_op jit(solution)/shard_map/reduce_scatter | solution.py:368
  348.4 425.0 %reduce-scatter.20.cloned.1.call-start = ((), (), s32[]{:S(2)}) async-start(), calls=%async_computation.15 | async-start | bytes 9732096 | tf_op jit(solution)/shard_map/reduce_scatter | solution.py:374
  383.7 515.0 %reduce-scatter.14.cloned.1.call-start = ((), (), s32[]{:S(2)}) async-start(), calls=%async_computation.12 | async-start | bytes 7299072 | tf_op jit(solution)/shard_map/reduce_scatter | solution.py:356
  (34 other events, 57.6 us)
Sparse Core Ops, SparseCore 0:
  64.4 29.8 all-gather.4
  96.4 27.2 all-gather.2
  221.5 26.3 reduce-scatter.7
  250.1 26.0 reduce-scatter.9
  281.9 99.1 reduce-scatter.15
  387.8 100.5 reduce-scatter.11
  495.8 134.7 reduce-scatter.17
  637.1 136.2 reduce-scatter.19
  780.6 118.0 reduce-scatter.13
